TPU v7x, 256 devices: a whole 4x4x8 slice. The times are simulated.
256 devices in a mesh: wide: 64 (over y, z, core), narrow: 4 (over x).
Axes of the slice: x: 4, y: 4, z: 8, core: 2. Of those that a mesh axis runs over, the one named last changes fastest.
Arguments:
- patches: bfloat16 [65536, 1280], P('wide', 'narrow'), may hold values from -6 to 6
- norm_gain: float32 [1280], replicated, may hold values from 0.1 to 1.9
- norm_bias: float32 [1280], replicated, may hold values from -3 to 3
- w_in: bfloat16 [1280, 5120], P('wide', 'narrow'), may hold values from -0.15625 to 0.15625
- b_in: float32 [5120], P('narrow'), may hold values from -3 to 3
- w_out: bfloat16 [5120, 1280], P('narrow', 'wide'), may hold values from -0.078125 to 0.078125
- b_out: float32 [1280], P('narrow'), may hold values from -3 to 3
- w_proj: bfloat16 [4, 1280, 1280], P(None, 'narrow', 'wide'), may hold values from -0.078125 to 0.078125
- b_proj: float32 [1280], P('narrow'), may hold values from -3 to 3
- text: bfloat16 [32768, 1280], P('wide', 'narrow'), may hold values from -6 to 6
- place: int32 [16384], replicated, may hold values from -1 to 32767, as said below
Outputs:
- prompt_embeds: bfloat16 [32768, 1280], P('wide', 'narrow')
Inputs may be any that keep to these rules, and one draw needn't show every extreme that they name: `place`: of the 256 entries of one wide index (entries i * 256 to (i + 1) * 256 - 1), the valid ones (>= 0) come first and -1 fills the rest; three quarters or more are valid, and all are valid for some wide index. Valid values are distinct. For one wide index, at most 8 valid entries v have the same v // 512, and every wide index reaches 8 for some value.
All inputs are finite; a program needn't handle non-finite values.
Results may differ from a plain program's by a relative error of at most 0.012.
Values may be sent and summed in bfloat16 or wider, within the bound.
A program may use at most 64 MiB of HBM per device.

v0:
```python
import jax
import jax.numpy as jnp
from jax import lax
from jax.sharding import PartitionSpec as P


def per_device(
    patches, norm_gain, norm_bias, w_in, b_in, w_out, b_out, w_proj, b_proj, text, place
):
    whole = lax.all_gather(patches, "narrow", axis=1, tiled=True)
    values = whole.astype(jnp.float32)
    center = jnp.mean(values, axis=-1, keepdims=True)
    spread = jnp.mean(jnp.square(values - center), axis=-1, keepdims=True)
    normed = ((values - center) * lax.rsqrt(spread + 1e-06) * norm_gain + norm_bias).astype(
        jnp.bfloat16
    )
    rows_in, cols_out, proj_cols = (
        lax.all_gather(w_in, "wide", axis=0, tiled=True),
        lax.all_gather(w_out, "wide", axis=1, tiled=True),
        lax.all_gather(w_proj, "wide", axis=2, tiled=True),
    )
    product = jnp.dot(normed, rows_in, preferred_element_type=jnp.float32)
    hidden = jax.nn.gelu(product + b_in, approximate=False).astype(jnp.bfloat16)
    partial_out = jnp.dot(hidden, cols_out, preferred_element_type=jnp.float32)
    mlp_out = lax.psum_scatter(
        partial_out.astype(jnp.bfloat16), "narrow", scatter_dimension=1, tiled=True
    ).astype(jnp.float32)
    stream = (patches.astype(jnp.float32) + (mlp_out + b_out)).astype(jnp.bfloat16)
    merge_count = stream.shape[0] // 4
    merged = stream.reshape(merge_count, 4 * stream.shape[1])
    groups = lax.axis_size("wide")
    own_index = lax.axis_index("wide")
    seq_rows = text.shape[0]
    bucket = seq_rows // groups
    place_table = place.reshape(groups, merge_count)
    owners = jnp.where(place_table >= 0, place_table // seq_rows, groups)
    own_owners = lax.dynamic_index_in_dim(owners, own_index, 0, keepdims=False)
    owner_hits = (own_owners[:, None] == jnp.arange(groups, dtype=jnp.int32)[None, :]).astype(
        jnp.int32
    )
    slot_out = jnp.sum(jnp.cumsum(owner_hits, axis=0) * owner_hits, axis=1) - 1
    slot_out = jnp.where(own_owners < groups, slot_out, bucket)
    arriving = owners == own_index
    slot_in = jnp.cumsum(arriving.astype(jnp.int32), axis=1) - 1
    slot_in = jnp.where(arriving, slot_in, bucket)
    local_row = jnp.where(arriving, place_table % seq_rows, seq_rows)
    source_ids = jnp.arange(groups, dtype=jnp.int32)[:, None]
    targets = (
        jnp.full((groups, bucket), seq_rows, jnp.int32)
        .at[source_ids, slot_in]
        .set(local_row, mode="drop")
    )
    partial_proj = jnp.dot(
        merged, proj_cols.reshape(-1, proj_cols.shape[2]), preferred_element_type=jnp.float32
    )
    vision = (
        lax.psum_scatter(
            partial_proj.astype(jnp.bfloat16), "narrow", scatter_dimension=1, tiled=True
        ).astype(jnp.float32)
        + b_proj
    ).astype(jnp.bfloat16)
    buffer = jnp.zeros((groups, bucket, vision.shape[1]), vision.dtype)
    received = lax.all_to_all(
        buffer.at[own_owners, slot_out].set(vision, mode="drop"),
        "wide",
        split_axis=0,
        concat_axis=0,
        tiled=True,
    )
    return text.at[targets.reshape(-1)].set(received.reshape(-1, received.shape[2]), mode="drop")


def solution(mesh):
    placed = (
        P("wide", "narrow"),
        P(),
        P(),
        P("wide", "narrow"),
        P("narrow"),
        P("narrow", "wide"),
        P("narrow"),
        P(None, "narrow", "wide"),
        P("narrow"),
        P("wide", "narrow"),
        P(),
    )
    return jax.shard_map(
        per_device, mesh=mesh, in_specs=placed, out_specs=P("wide", "narrow"), check_vma=False
    )
```

profile of v0, /device:TPU:1, one launch (start us, length us, event | category | flops | bytes accessed | tf_op | source)
XLA Modules:
  0.0 475.5 jit_solution(18074952579770676036)
XLA Ops:
  6.5 0.7 all-gather.7.cloned.1.call-update
  7.3 0.7 all-gather.13.cloned.1.call-update
  8.1 0.7 all-gather.11.cloned.1.call-update
  8.8 0.5 all-gather.9.cloned.1.call-update
  9.3 0.0 reduce-scatter.3.cloned.1.call-start
  9.4 41.4 %all-gather.7.cloned.1.call-done = bf16[1024,1280]{0,1:T(8,128)(2,1)} async-done(((bf16[1024,320]{0,1:T(8,128)(2,1)}), bf16[1024,1280]{0,1:T(8,128)(2,1)}) %all-gather.7.cloned.1.call-update) | async-done | bytes 2621456 | tf_op jit(solution)/shard_map/all_gather | solution.py:10
  50.7 2.3 convert_reduce_fusion
  53.1 0.2 copy-done
  53.2 0.7 fusion.2
  54.0 78.9 %all-gather.13.cloned.1.call-done = bf16[64,20,1280]{2,1,0:T(8,128)(2,1)} async-done(((bf16[1,20,1280]{2,1,0:T(8,128)(2,1)}), bf16[64,20,1280]{2,1,0:T(8,128)(2,1)}) %all-gather.13.cloned.1.call-update) | async-done | bytes 3276816 | tf_op jit(solution)/shard_map/all_gather | solution.py:19
  132.9 6.1 %reshape.317 = bf16[1280,1280]{1,0:T(8,128)(2,1)} reshape(bf16[64,20,1280]{2,1,0:T(8,128)(2,1)} %all-gather.13.cloned.1.call-done) | data formatting | bytes 6553600
  139.1 72.6 %all-gather.11.cloned.1.call-done = bf16[64,20,1280]{2,1,0:T(8,128)(2,1)} async-done(((bf16[1,20,1280]{2,1,0:T(8,128)(2,1)}), bf16[64,20,1280]{2,1,0:T(8,128)(2,1)}) %all-gather.11.cloned.1.call-update) | async-done | bytes 3276816 | tf_op jit(solution)/shard_map/all_gather | solution.py:18
  211.7 6.1 %reshape.315 = bf16[1280,1280]{1,0:T(8,128)(2,1)} reshape(bf16[64,20,1280]{2,1,0:T(8,128)(2,1)} %all-gather.11.cloned.1.call-done) | data formatting | bytes 6553600
  217.8 21.4 %convolution_convert_fusion = bf16[1024,1280]{0,1:T(8,128)(2,1)} fusion(bf16[1280,1280]{1,0:T(8,128)(2,1)} %reshape.317, bf16[1280,1280]{1,0:T(8,128)(2,1)} %reshape.315, bf16[1024,1280]{0,1:T(8,128)(2,1)S(1)} %copy-done, f32[1280]{0:T(1024)S(1)} %copy-done.6, f32[1280]{0:T(1024)S(1)} %copy-done.7, f32[1280]{0:T(1024)S(1)} %copy-done.8, ...), kind=kOutput, calls=%fused_computation.30 | convolution fusion | flops 6806568960 | bytes 11820032 | tf_op jit(solution)/shard_map/dot_general | solution.py:24
  239.3 0.0 reduce-scatter.5.cloned.1.call-start
  239.4 0.1 fusion.40
  239.4 0.6 reduce-window.14
  240.0 0.2 slice_reduce_fusion.1
  240.3 0.1 add_add_fusion
  240.4 49.9 %all-gather.9.cloned.1.call-done = bf16[4,320,1280]{1,0,2:T(4,128)(2,1)} async-done(((bf16[4,320,20]{1,0,2:T(4,128)(2,1)}), bf16[4,320,1280]{1,0,2:T(4,128)(2,1)}) %all-gather.9.cloned.1.call-update) | async-done | bytes 3276816 | tf_op jit(solution)/shard_map/all_gather | solution.py:20
  290.3 7.3 %copy.46 = bf16[4,320,1280]{2,1,0:T(8,128)(2,1)S(1)} copy(bf16[4,320,1280]{1,0,2:T(4,128)(2,1)} %all-gather.9.cloned.1.call-done) | data formatting | bytes 6553600 | tf_op jit(solution)/shard_map/all_gather | solution.py:20
  297.6 28.3 %reduce-scatter.3.cloned.1.call-done = bf16[1024,320]{0,1:T(8,128)(2,1)} async-done(((bf16[1024,1280]{0,1:T(8,128)(2,1)}), bf16[1024,320]{0,1:T(8,128)(2,1)}) %reduce-scatter.3.cloned.1.call-update) | async-done | bytes 655376 | tf_op jit(solution)/shard_map/reduce_scatter | solution.py:25
  326.0 2.4 add_convert_fusion
  328.4 2.2 copy.45
  330.6 2.5 reshape.287
  333.1 3.3 convolution_convert_fusion.1
  336.4 0.1 fusion.31
  336.5 1.2 copy.48
  337.7 0.1 copy.42
  337.8 0.1 sub.37
  337.9 0.6 reduce-window.16
  338.5 0.2 slice_reduce_fusion
  338.7 0.1 fusion.35
  338.9 0.1 compare_select_fusion
  338.9 20.6 %reduce-scatter.5.cloned.1.call-done = bf16[256,320]{0,1:T(8,128)(2,1)} async-done(((bf16[256,1280]{0,1:T(8,128)(2,1)}), bf16[256,320]{0,1:T(8,128)(2,1)}) %reduce-scatter.5.cloned.1.call-update) | async-done | bytes 163856 | tf_op jit(solution)/shard_map/reduce_scatter | solution.py:57
  359.5 1.0 add_convert_fusion.1
  360.5 0.2 copy.47
  360.7 0.8 broadcast_in_dim.47
  361.5 30.9 %scatter_fusion = bf16[64,8,320]{2,1,0:T(8,128)(2,1)} fusion(bf16[64,8,320]{2,1,0:T(8,128)(2,1)} %broadcast_in_dim.47, s32[256]{0:T(256)S(1)} %bitcast.42, bf16[256,320]{1,0:T(8,128)(2,1)S(1)} %copy.47), kind=kCustom, calls=%fused_computation | custom fusion | bytes 493568 | tf_op jit(solution)/shard_map/scatter | solution.py:64
  392.4 11.9 %all-to-all-start = ((bf16[64,8,320]{2,1,0:T(8,128)(2,1)}), bf16[64,8,320]{2,1,0:T(8,128)(2,1)S(1)}, u32[]{:S(2)}, u32[]{:S(2)}) async-start(bf16[64,8,320]{2,1,0:T(8,128)(2,1)} %scatter_fusion), calls=%async_computation.2 | async-start | bytes 786432 | tf_op jit(solution)/shard_map/all_to_all | solution.py:63
  404.3 0.1 multiply_reduce_fusion
  404.4 0.1 and_reduce_fusion
  404.6 60.3 %scatter_custom_fusion.2 = s32[512]{0:T(512)S(1)} fusion(s32[16384]{0:T(1024)S(1)} %bitcast.45, s32[16384]{0:T(1024)S(1)} %bitcast.46, s32[]{:T(128)} %constant.43.clone.1), kind=kCustom, calls=%fused_computation.95 | custom fusion | bytes 2052
  464.9 0.1 reshape.292
  465.0 0.1 copy.43
  465.0 0.1 reshape.285
  465.2 2.6 scatter_custom_fusion.1
  467.7 0.9 copy.49
  (41 shorter events, 0.5 us)
Async XLA Ops:
  6.5 44.2 %all-gather.7.cloned.1.call-start = ((), (), s32[]{:S(2)}) async-start(), calls=%async_computation.3 | async-start | bytes 3276800 | tf_op jit(solution)/shard_map/all_gather | solution.py:10
  7.3 125.7 %all-gather.13.cloned.1.call-start = ((), (), s32[]{:S(2)}) async-start(), calls=%async_computation.8 | async-start | bytes 3993600 | tf_op jit(solution)/shard_map/all_gather | solution.py:19
  8.0 203.7 %all-gather.11.cloned.1.call-start = ((), (), s32[]{:S(2)}) async-start(), calls=%async_computation.7 | async-start | bytes 3993600 | tf_op jit(solution)/shard_map/all_gather | solution.py:18
  8.7 281.6 %all-gather.9.cloned.1.call-start = ((), (), s32[]{:S(2)}) async-start(), calls=%async_computation.5 | async-start | bytes 3993600 | tf_op jit(solution)/shard_map/all_gather | solution.py:20
  9.3 316.6 %reduce-scatter.3.cloned.1.call-start = ((), (), s32[]{:S(2)}) async-start(), calls=%async_computation.4 | async-start | bytes 3276800 | tf_op jit(solution)/shard_map/reduce_scatter | solution.py:25
  50.7 2.5 copy-start
  139.1 78.8 %copy-start.6 = (f32[1280]{0:T(1024)S(1)}, f32[1280]{0:T(1024)}, u32[]{:S(2)}) copy-start(f32[1280]{0:T(1024)} %param.15) | copy-start | bytes 15364
  139.1 78.8 %copy-start.7 = (f32[1280]{0:T(1024)S(1)}, f32[1280]{0:T(1024)}, u32[]{:S(2)}) copy-start(f32[1280]{0:T(1024)} %param.13) | copy-start | bytes 15364
  139.1 78.8 %copy-start.8 = (f32[1280]{0:T(1024)S(1)}, f32[1280]{0:T(1024)}, u32[]{:S(2)}) copy-start(f32[1280]{0:T(1024)} %param.12) | copy-start | bytes 15364
  217.8 21.5 %copy-start.1 = (s32[16384]{0:T(1024)S(1)}, s32[16384]{0:T(1024)}, u32[]{:S(2)}) copy-start(s32[16384]{0:T(1024)} %param.21) | copy-start | bytes 196612
  239.2 86.7 %copy-start.2 = (f32[320]{0:T(512)S(1)}, f32[320]{0:T(512)}, u32[]{:S(2)}) copy-start(f32[320]{0:T(512)} %param.17) | copy-start | bytes 3844
  239.3 120.2 %reduce-scatter.5.cloned.1.call-start = ((), (), s32[]{:S(2)}) async-start(), calls=%async_computation.6 | async-start | bytes 819200 | tf_op jit(solution)/shard_map/reduce_scatter | solution.py:57
  333.1 26.4 %copy-start.3 = (f32[320]{0:T(512)S(1)}, f32[320]{0:T(512)}, u32[]{:S(2)}) copy-start(f32[320]{0:T(512)} %param.19) | copy-start | bytes 3844
  336.4 67.9 %copy-start.5 = (s32[2]{0:T(128)S(1)}, s32[2]{0:T(128)}, u32[]{:S(2)}) copy-start(s32[2]{0:T(128)} %constant.137) | copy-start | bytes 28
  336.4 68.0 %copy-start.4 = (s32[2]{0:T(128)S(1)}, s32[2]{0:T(128)}, u32[]{:S(2)}) copy-start(s32[2]{0:T(128)} %constant.140) | copy-start | bytes 28
  392.4 72.8 %all-to-all-start = ((bf16[64,8,320]{2,1,0:T(8,128)(2,1)}), bf16[64,8,320]{2,1,0:T(8,128)(2,1)S(1)}, u32[]{:S(2)}, u32[]{:S(2)}) async-start(bf16[64,8,320]{2,1,0:T(8,128)(2,1)} %scatter_fusion), calls=%async_computation.2 | async-start | bytes 786432 | tf_op jit(solution)/shard_map/all_to_all | solution.py:63
Sparse Core Ops, SparseCore 0:
  9.2 41.5 all-gather.6
  53.4 79.4 all-gather.12
  135.6 76.0 all-gather.10
  214.3 75.9 all-gather.8
  292.7 33.2 reduce-scatter.2
  336.5 22.9 reduce-scatter.4
where the time goes:
time: 477 us; the launch traced here: 475 us
  waiting for transfers between devices  294 us (62%)
  local copies, waits for them, and re-layouts  122 us (26%)
  matrix products  24.7 us (5%)
  between operations  13.7 us (3%)
  starting transfers between devices  12.1 us (3%)
  other arithmetic  8.4 us (2%)
    all_gather x1, waiting for transfers between devices, per_device(): lax.all_gather(w_out, 'wide', axis=1, tiled=True)  78.9 us
    unnamed x25, local copies, waits for them, and re-layouts  74.1 us
    all_gather x1, waiting for transfers between devices, per_device(): lax.all_gather(w_in, 'wide', axis=0, tiled=True)  72.6 us
    all_gather x1, waiting for transfers between devices, per_device(): lax.all_gather(w_proj, 'wide', axis=2, tiled=True)  49.9 us
    all_gather x1, waiting for transfers between devices, per_device(): whole = lax.all_gather(patches, 'narrow', axis=1, tiled=True)  41.4 us
    scatter x1, local copies, waits for them, and re-layouts, per_device(): buffer.at[own_owners, slot_out].set(vision, mode='drop')  30.9 us
    reduce_scatter x1, waiting for transfers between devices, per_device(): lax.psum_scatter(partial_out.astype(jnp.bfloat16), 'narrow', scatter_dime...  28.3 us
    dot_general x1, matrix products, per_device(): partial_out = jnp.dot(hidden, cols_out, preferred_element_type=jnp.float32)  21.4 us
  transfers between devices with their start and end apart: 7, of which 6 were waited for; matrix products, arithmetic and copies ran while one was open for 23% of the time, Pallas kernels for 0%

commit v1 on v0

--- a/solution.py
+++ b/solution.py
@@ -7,7 +7,14 @@
 def per_device(
     patches, norm_gain, norm_bias, w_in, b_in, w_out, b_out, w_proj, b_proj, text, place
 ):
-    whole = lax.all_gather(patches, "narrow", axis=1, tiled=True)
+    ring = [patches]
+    for hop in range(3):
+        ring.append(lax.ppermute(ring[-1], "narrow", [(dev, (dev + 1) % 4) for dev in range(4)]))
+    whole = jnp.roll(
+        jnp.concatenate(ring[::-1], axis=1),
+        (lax.axis_index("narrow") + 1) * ring[0].shape[1],
+        axis=1,
+    )
     values = whole.astype(jnp.float32)
     center = jnp.mean(values, axis=-1, keepdims=True)
     spread = jnp.mean(jnp.square(values - center), axis=-1, keepdims=True)

time: 477 us -> 434 us (0.910)
  waiting for transfers between devices: 294 us -> 248 us
  starting transfers between devices: 12.1 us -> 17 us
    all_gather x1 -> x0, waiting for transfers between devices: 41.4 us -> none  [per_device(): whole = lax.all_gather(patches, 'narrow', axis=1, tiled=True)]
    ppermute x0 -> x3, waiting for transfers between devices: none -> 40.1 us  [per_device(): lax.ppermute(ring[-1], 'narrow', [(dev, (dev + 1) % 4) for dev in range(4)])]
    all_gather x1, waiting for transfers between devices: 72.6 us -> 35.1 us  [per_device(): lax.all_gather(w_in, 'wide', axis=0, tiled=True)]
    all_gather x1, waiting for transfers between devices: 78.9 us -> 72.7 us  [per_device(): lax.all_gather(w_out, 'wide', axis=1, tiled=True)]
    ppermute x0 -> x3, starting transfers between devices: none -> 4.95 us  [per_device(): lax.ppermute(ring[-1], 'narrow', [(dev, (dev + 1) % 4) for dev in range(4)])]
    unnamed x25 -> x38, local copies, waits for them, and re-layouts: 74.1 us -> 75.8 us
  transfers between devices with their start and end apart: 7 -> 9, of which waited for: 6 -> 8; matrix products, arithmetic and copies ran while one was open for 23% -> 25% of each run, Pallas kernels for 0% -> 0%
where the time goes in v1:
time: 434 us; the launch traced here: 432 us
  waiting for transfers between devices  248 us (57%)
  local copies, waits for them, and re-layouts  121 us (28%)
  matrix products  26.4 us (6%)
  starting transfers between devices  17 us (4%)
  between operations  13.6 us (3%)
  other arithmetic  6.12 us (1%)
    unnamed x38, local copies, waits for them, and re-layouts  75.8 us
    all_gather x1, waiting for transfers between devices, per_device(): lax.all_gather(w_out, 'wide', axis=1, tiled=True)  72.7 us
    all_gather x1, waiting for transfers between devices, per_device(): lax.all_gather(w_proj, 'wide', axis=2, tiled=True)  49.3 us
    ppermute x3, waiting for transfers between devices, per_device(): lax.ppermute(ring[-1], 'narrow', [(dev, (dev + 1) % 4) for dev in range(4)])  40.1 us
    all_gather x1, waiting for transfers between devices, per_device(): lax.all_gather(w_in, 'wide', axis=0, tiled=True)  35.1 us
    scatter x1, local copies, waits for them, and re-layouts, per_device(): buffer.at[own_owners, slot_out].set(vision, mode='drop')  30.9 us
    reduce_scatter x1, waiting for transfers between devices, per_device(): lax.psum_scatter(partial_out.astype(jnp.bfloat16), 'narrow', scatter_dime...  27.9 us
    dot_general x1, matrix products, per_device(): partial_out = jnp.dot(hidden, cols_out, preferred_element_type=jnp.float32)  22.2 us
  transfers between devices with their start and end apart: 9, of which 8 were waited for; matrix products, arithmetic and copies ran while one was open for 25% of the time, Pallas kernels for 0%

profile of v1, /device:TPU:1, one launch (start us, length us, event | category | flops | bytes accessed | tf_op | source)
XLA Modules:
  0.0 432.0 jit_solution(1523848726433789980)
XLA Ops:
  6.5 0.7 all-gather.8.cloned.1.call-update
  7.3 0.7 all-gather.10.cloned.1.call-update
  8.1 2.1 collective-permute-start
  10.2 13.6 %collective-permute-done = bf16[1024,320]{0,1:T(8,128)(2,1)S(1)} collective-permute-done((bf16[1024,320]{0,1:T(8,128)(2,1)}, bf16[1024,320]{0,1:T(8,128)(2,1)S(1)}, u32[]{:S(2)}, u32[]{:S(2)}) %collective-permute-start) | collective-permute-done | bytes 655392 | tf_op jit(solution)/shard_map/ppermute | solution.py:12
  23.8 1.9 collective-permute-start.1
  25.7 13.6 %collective-permute-done.1 = bf16[1024,320]{0,1:T(8,128)(2,1)S(1)} collective-permute-done((bf16[1024,320]{0,1:T(8,128)(2,1)S(1)}, bf16[1024,320]{0,1:T(8,128)(2,1)S(1)}, u32[]{:S(2)}, u32[]{:S(2)}) %collective-permute-start.1) | collective-permute-done | bytes 655392 | tf_op jit(solution)/shard_map/ppermute | solution.py:12
  39.2 0.9 collective-permute-start.2
  40.3 12.9 %collective-permute-done.2 = bf16[1024,320]{0,1:T(8,128)(2,1)S(1)} collective-permute-done((bf16[1024,320]{0,1:T(8,128)(2,1)S(1)}, bf16[1024,320]{0,1:T(8,128)(2,1)S(1)}, u32[]{:S(2)}, u32[]{:S(2)}) %collective-permute-start.2) | collective-permute-done | bytes 655392 | tf_op jit(solution)/shard_map/ppermute | solution.py:12
  53.4 1.1 constant_dynamic-update-slice_fusion.4
  54.7 0.8 convert_reduce_fusion
  55.5 1.5 copy-done
  57.0 1.1 fusion.2
  58.1 35.1 %all-gather.8.cloned.1.call-done = bf16[64,20,1280]{2,1,0:T(8,128)(2,1)} async-done(((bf16[1,20,1280]{2,1,0:T(8,128)(2,1)}), bf16[64,20,1280]{2,1,0:T(8,128)(2,1)}) %all-gather.8.cloned.1.call-update) | async-done | bytes 3276816 | tf_op jit(solution)/shard_map/all_gather | solution.py:25
  93.2 6.1 %reshape.315 = bf16[1280,1280]{1,0:T(8,128)(2,1)} reshape(bf16[64,20,1280]{2,1,0:T(8,128)(2,1)} %all-gather.8.cloned.1.call-done) | data formatting | bytes 6553600
  99.3 72.7 %all-gather.10.cloned.1.call-done = bf16[64,20,1280]{2,1,0:T(8,128)(2,1)} async-done(((bf16[1,20,1280]{2,1,0:T(8,128)(2,1)}), bf16[64,20,1280]{2,1,0:T(8,128)(2,1)}) %all-gather.10.cloned.1.call-update) | async-done | bytes 3276816 | tf_op jit(solution)/shard_map/all_gather | solution.py:26
  172.0 6.1 %reshape.317 = bf16[1280,1280]{1,0:T(8,128)(2,1)} reshape(bf16[64,20,1280]{2,1,0:T(8,128)(2,1)} %all-gather.10.cloned.1.call-done) | data formatting | bytes 6553600
  178.1 22.2 %convolution_convert_fusion = bf16[1024,1280]{0,1:T(8,128)(2,1)} fusion(bf16[1280,1280]{1,0:T(8,128)(2,1)} %reshape.317, bf16[1280,1280]{1,0:T(8,128)(2,1)} %reshape.315, f32[1280]{0:T(1024)S(1)} %copy-done.9, f32[1280]{0:T(1024)S(1)} %copy-done.10, f32[1280]{0:T(1024)S(1)} %copy-done.11, f32[1024]{0:T(1024)S(1)} %add_rsqrt_fusion, ...), kind=kOutput, calls=%fused_computation.30 | convolution fusion | flops 6806568960 | bytes 11820036 | tf_op jit(solution)/shard_map/dot_general | solution.py:31
  200.5 0.1 fusion.33
  200.6 0.6 reduce-window.16
  201.2 0.2 slice_reduce_fusion
  201.4 49.3 %all-gather.6.cloned.1.call-done = bf16[4,320,1280]{1,0,2:T(4,128)(2,1)} async-done(((bf16[4,320,20]{1,0,2:T(4,128)(2,1)}), bf16[4,320,1280]{1,0,2:T(4,128)(2,1)}) %all-gather.6.cloned.1.call-update) | async-done | bytes 3276816 | tf_op jit(solution)/shard_map/all_gather | solution.py:27
  250.7 7.8 %copy.46 = bf16[4,320,1280]{2,1,0:T(8,128)(2,1)} copy(bf16[4,320,1280]{1,0,2:T(4,128)(2,1)} %all-gather.6.cloned.1.call-done) | data formatting | bytes 6553600 | tf_op jit(solution)/shard_map/all_gather | solution.py:27
  258.5 27.9 %reduce-scatter.3.cloned.1.call-done = bf16[1024,320]{0,1:T(8,128)(2,1)} async-done(((bf16[1024,1280]{0,1:T(8,128)(2,1)}), bf16[1024,320]{0,1:T(8,128)(2,1)}) %reduce-scatter.3.cloned.1.call-update) | async-done | bytes 655376 | tf_op jit(solution)/shard_map/reduce_scatter | solution.py:32
  286.4 1.3 add_convert_fusion
  287.8 0.4 copy.45
  288.2 0.7 reshape.287
  288.9 4.2 convolution_convert_fusion.1
  293.1 0.6 reduce-window.14
  293.8 0.2 slice_reduce_fusion.1
  294.0 0.1 add_add_fusion
  294.1 0.1 sub.41
  294.2 0.1 fusion.37
  294.3 0.1 compare_select_fusion
  294.4 21.7 %reduce-scatter.5.cloned.1.call-done = bf16[256,320]{0,1:T(8,128)(2,1)} async-done(((bf16[256,1280]{0,1:T(8,128)(2,1)}), bf16[256,320]{0,1:T(8,128)(2,1)}) %reduce-scatter.5.cloned.1.call-update) | async-done | bytes 163856 | tf_op jit(solution)/shard_map/reduce_scatter | solution.py:64
  316.1 1.0 add_convert_fusion.1
  317.2 0.2 copy.47
  317.3 0.8 broadcast_in_dim.47
  318.1 30.9 %scatter_fusion = bf16[64,8,320]{2,1,0:T(8,128)(2,1)} fusion(bf16[64,8,320]{2,1,0:T(8,128)(2,1)} %broadcast_in_dim.47, s32[256]{0:T(256)S(1)} %bitcast.42, bf16[256,320]{1,0:T(8,128)(2,1)S(1)} %copy.47), kind=kCustom, calls=%fused_computation | custom fusion | bytes 493568 | tf_op jit(solution)/shard_map/scatter | solution.py:71
  349.0 11.9 %all-to-all-start = ((bf16[64,8,320]{2,1,0:T(8,128)(2,1)}), bf16[64,8,320]{2,1,0:T(8,128)(2,1)S(1)}, u32[]{:S(2)}, u32[]{:S(2)}) async-start(bf16[64,8,320]{2,1,0:T(8,128)(2,1)} %scatter_fusion), calls=%async_computation.2 | async-start | bytes 786432 | tf_op jit(solution)/shard_map/all_to_all | solution.py:70
  360.9 0.1 multiply_reduce_fusion
  361.0 0.1 and_reduce_fusion
  361.2 60.3 %scatter_custom_fusion.2 = s32[512]{0:T(512)S(1)} fusion(s32[16384]{0:T(1024)S(1)} %bitcast.45, s32[16384]{0:T(1024)S(1)} %bitcast.46, s32[]{:T(128)} %constant.47.clone.1), kind=kCustom, calls=%fused_computation.104 | custom fusion | bytes 2052
  421.5 0.1 reshape.292
  421.6 0.1 copy.43
  421.7 0.1 reshape.285
  421.8 0.2 copy.48
  422.0 2.6 scatter_custom_fusion.1
  424.6 0.9 copy.49
  (59 shorter events, 1.0 us)
Async XLA Ops:
  6.5 48.1 %copy-start.1 = (bf16[1024,320]{0,1:T(8,128)(2,1)S(1)}, bf16[1024,320]{0,1:T(8,128)(2,1)}, u32[]{:S(2)}) copy-start(bf16[1024,320]{0,1:T(8,128)(2,1)} %param.11) | copy-start | bytes 1966084
  6.5 86.7 %all-gather.8.cloned.1.call-start = ((), (), s32[]{:S(2)}) async-start(), calls=%async_computation.6 | async-start | bytes 3993600 | tf_op jit(solution)/shard_map/all_gather | solution.py:25
  7.3 164.7 %all-gather.10.cloned.1.call-start = ((), (), s32[]{:S(2)}) async-start(), calls=%async_computation.7 | async-start | bytes 3993600 | tf_op jit(solution)/shard_map/all_gather | solution.py:26
  8.0 242.7 %all-gather.6.cloned.1.call-start = ((), (), s32[]{:S(2)}) async-start(), calls=%async_computation.4 | async-start | bytes 3993600 | tf_op jit(solution)/shard_map/all_gather | solution.py:27
  8.1 15.8 %collective-permute-start = (bf16[1024,320]{0,1:T(8,128)(2,1)}, bf16[1024,320]{0,1:T(8,128)(2,1)S(1)}, u32[]{:S(2)}, u32[]{:S(2)}) collective-permute-start(bf16[1024,320]{0,1:T(8,128)(2,1)} %param.11), channel_id=1, source_target_pairs={{0,1},{1,2},{2,3},{3,0},{4,5},{5,6},{6,7},{7,4},{8,9},{9,10},{10,1... | collective-permute-start | bytes 1966088 | tf_op jit(solution)/shard_map/ppermute | solution.py:12
  23.8 15.4 %collective-permute-start.1 = (bf16[1024,320]{0,1:T(8,128)(2,1)S(1)}, bf16[1024,320]{0,1:T(8,128)(2,1)S(1)}, u32[]{:S(2)}, u32[]{:S(2)}) collective-permute-start(bf16[1024,320]{0,1:T(8,128)(2,1)S(1)} %collective-permute-done), channel_id=1, source_target_pairs={{0,1},{1,2},{2,3},{3,0},{4,5},{5,6},{6,7},{7,4},{8,9},{9,10},{10,1... | collective-permute-start | bytes 1966088 | tf_op jit(solution)/shard_map/ppermute | solution.py:12
  39.2 14.0 %collective-permute-start.2 = (bf16[1024,320]{0,1:T(8,128)(2,1)S(1)}, bf16[1024,320]{0,1:T(8,128)(2,1)S(1)}, u32[]{:S(2)}, u32[]{:S(2)}) collective-permute-start(bf16[1024,320]{0,1:T(8,128)(2,1)S(1)} %collective-permute-done.1), channel_id=1, source_target_pairs={{0,1},{1,2},{2,3},{3,0},{4,5},{5,6},{6,7},{7,4},{8,9},{9,10},{10,1... | collective-permute-start | bytes 1966088 | tf_op jit(solution)/shard_map/ppermute | solution.py:12
  40.2 246.2 %reduce-scatter.3.cloned.1.call-start = ((), (), s32[]{:S(2)}) async-start(), calls=%async_computation.3 | async-start | bytes 3276800 | tf_op jit(solution)/shard_map/reduce_scatter | solution.py:32
  54.7 2.3 copy-start
  99.3 78.8 %copy-start.9 = (f32[1280]{0:T(1024)S(1)}, f32[1280]{0:T(1024)}, u32[]{:S(2)}) copy-start(f32[1280]{0:T(1024)} %param.15) | copy-start | bytes 15364
  99.3 78.8 %copy-start.10 = (f32[1280]{0:T(1024)S(1)}, f32[1280]{0:T(1024)}, u32[]{:S(2)}) copy-start(f32[1280]{0:T(1024)} %param.13) | copy-start | bytes 15364
  99.3 78.8 %copy-start.11 = (f32[1280]{0:T(1024)S(1)}, f32[1280]{0:T(1024)}, u32[]{:S(2)}) copy-start(f32[1280]{0:T(1024)} %param.12) | copy-start | bytes 15364
  178.1 22.3 %copy-start.2 = (s32[16384]{0:T(1024)S(1)}, s32[16384]{0:T(1024)}, u32[]{:S(2)}) copy-start(s32[16384]{0:T(1024)} %param.21) | copy-start | bytes 196612
  200.3 86.1 %copy-start.5 = (f32[320]{0:T(512)S(1)}, f32[320]{0:T(512)}, u32[]{:S(2)}) copy-start(f32[320]{0:T(512)} %param.17) | copy-start | bytes 3844
  200.3 115.8 %reduce-scatter.5.cloned.1.call-start = ((), (), s32[]{:S(2)}) async-start(), calls=%async_computation.5 | async-start | bytes 819200 | tf_op jit(solution)/shard_map/reduce_scatter | solution.py:64
  201.4 86.7 %copy-start.4 = (s32[64,3]{0,1:T(4,128)}, s32[64,3]{0,1:T(4,128)S(1)}, u32[]{:S(2)}) copy-start(s32[64,3]{0,1:T(4,128)S(1)} %reduce-window.19) | copy-start | bytes 2308
  287.8 28.4 %copy-start.6 = (f32[320]{0:T(512)S(1)}, f32[320]{0:T(512)}, u32[]{:S(2)}) copy-start(f32[320]{0:T(512)} %param.19) | copy-start | bytes 3844
  288.9 5.3 %slice-start = ((s32[64,3]{0,1:T(4,128)}), s32[64,2]{0,1:T(2,128)S(1)}, s32[]{:S(2)}) async-start(s32[64,3]{0,1:T(4,128)} %copy-done.4), calls=%async_computation.8 | async-start | bytes 2048 | tf_op jit(solution)/shard_map/slice.3
  288.9 72.0 %copy-start.8 = (s32[2]{0:T(128)S(1)}, s32[2]{0:T(128)}, u32[]{:S(2)}) copy-start(s32[2]{0:T(128)} %constant.161) | copy-start | bytes 28
  288.9 72.1 %copy-start.7 = (s32[2]{0:T(128)S(1)}, s32[2]{0:T(128)}, u32[]{:S(2)}) copy-start(s32[2]{0:T(128)} %constant.164) | copy-start | bytes 28
  293.1 128.7 %copy-start.3 = (bf16[512,320]{0,1:T(8,128)(2,1)S(1)}, bf16[512,320]{0,1:T(8,128)(2,1)}, u32[]{:S(2)}) copy-start(bf16[512,320]{0,1:T(8,128)(2,1)} %param.20) | copy-start | bytes 983044
  349.0 73.0 %all-to-all-start = ((bf16[64,8,320]{2,1,0:T(8,128)(2,1)}), bf16[64,8,320]{2,1,0:T(8,128)(2,1)S(1)}, u32[]{:S(2)}, u32[]{:S(2)}) async-start(bf16[64,8,320]{2,1,0:T(8,128)(2,1)} %scatter_fusion), calls=%async_computation.2 | async-start | bytes 786432 | tf_op jit(solution)/shard_map/all_to_all | solution.py:70
Sparse Core Ops, SparseCore 0:
  10.0 83.1 all-gather.7
  95.9 76.0 all-gather.9
  174.7 76.0 all-gather.5
  253.1 33.2 reduce-scatter.2
  293.2 22.8 reduce-scatter.4
